TPU v7x, 512 devices: a whole 4x4x16 slice. The times are simulated.
512 devices in a mesh: blk: 128 (over z, x, core), col: 4 (over y).
Axes of the slice: x: 4, y: 4, z: 16, core: 2. Of those that a mesh axis runs over, the one named last changes fastest.
Arguments:
- upper_row: float32 [512, 128, 512], P(None, 'blk', 'col'), may hold values from -0.17 to 4.17, as said below
- lower_row: float32 [512, 128, 512], P(None, 'blk', 'col'), may hold values from -0.1 to 0.1
Outputs:
- new_upper: float32 [512, 128, 512], P(None, 'blk', 'col')
- new_lower: float32 [512, 128, 512], P(None, 'blk', 'col')
Inputs may be any that keep to these rules, and one draw needn't show every extreme that they name: Block 0 of upper_row is 4 times the identity plus entries within 0.16 of it; the other blocks hold entries within 0.1.
All inputs are finite; a program needn't handle non-finite values.
Results may differ from a plain program's by a relative error of at most 0.00023.
Values sent between devices are 32-bit elements; how exact they have to be, the bound alone decides.
A program may use at most 64 MiB of HBM per device.

v0:
```python
import jax
import jax.numpy as jnp
from jax import lax
from jax.sharding import PartitionSpec as P

HIGHEST_PREC = lax.Precision.HIGHEST


def shifted(value, axis, steps):
    count = lax.axis_size(axis)
    initial, last = (max(0, -steps), min(count, count - steps))
    return lax.ppermute(value, axis, [(source, source + steps) for source in range(initial, last)])


def broadcast(block, axis, holder):
    block = jnp.where(lax.axis_index(axis) == holder, block, jnp.zeros_like(block))
    return lax.psum(block, axis)


def product(left_mat, right_mat):
    return jnp.dot(left_mat, right_mat, precision=HIGHEST_PREC, preferred_element_type=jnp.float32)


def apply_rows(matrix, blocks):
    return jnp.einsum(
        "ij,jkc->ikc", matrix, blocks, precision=HIGHEST_PREC, preferred_element_type=jnp.float32
    )


def apply_transposed(matrix, blocks):
    return jnp.einsum(
        "ri,rkc->ikc", matrix, blocks, precision=HIGHEST_PREC, preferred_element_type=jnp.float32
    )


def gram_of(reflect):
    return jnp.einsum(
        "ri,rj->ij", reflect, reflect, precision=HIGHEST_PREC, preferred_element_type=jnp.float32
    )


def slide_upper(upper_row):
    incoming = shifted(upper_row, "blk", 1)
    return jnp.concatenate([incoming, upper_row[:, :-1, :]], axis=1)


def first_inverse(head_upper, identity):
    norm_scale = jnp.sqrt(jnp.sum(head_upper * head_upper) / head_upper.shape[0] + 1e-06)
    return (2.0 * identity - head_upper / norm_scale) / norm_scale


def transform_split(head_upper, head_lower, col_start, col_width):
    identity = jnp.eye(head_upper.shape[0], dtype=jnp.float32)
    identity_part = lax.dynamic_slice_in_dim(identity, col_start, col_width, 1)
    inverse_one = first_inverse(head_upper, identity)
    inverse_cols = lax.dynamic_slice_in_dim(inverse_one, col_start, col_width, 1)
    inverse_part = product(inverse_one, 2.0 * identity_part - product(head_upper, inverse_cols))
    reflect_part = product(head_lower, inverse_part)
    reflect = lax.all_gather(reflect_part, "col", axis=1, tiled=True)
    gram_matrix = gram_of(reflect)
    power_one = lax.dynamic_slice_in_dim(gram_matrix, col_start, col_width, 1)
    power_two = product(gram_matrix, power_one)
    power_three = product(gram_matrix, power_two)
    power_four = product(gram_matrix, power_three)
    left_part = (
        identity_part
        + 0.5 * power_one
        + 0.375 * power_two
        + 0.3125 * power_three
        + 0.0625 * power_four
    )
    inner_part = 0.5 * identity_part + 0.375 * power_one + 0.3125 * power_two + 0.0625 * power_three
    left_root, inner_poly = (
        lax.all_gather(left_part, "col", axis=1, tiled=True),
        lax.all_gather(inner_part, "col", axis=1, tiled=True),
    )
    return (reflect, left_root, inner_poly)


def shards(upper_row, lower_row):
    blocks_here = upper_row.shape[1]
    col_width = upper_row.shape[2]
    col_start = lax.axis_index("col") * col_width
    root_index = 1 // blocks_here
    local_index = 1 % blocks_here
    upper_row = slide_upper(upper_row)
    lead_upper = broadcast(upper_row[:, local_index, :], "blk", root_index)
    lead_lower = broadcast(lower_row[:, local_index, :], "blk", root_index)
    head_upper = lax.all_gather(lead_upper, "col", axis=1, tiled=True)
    head_lower = lax.all_gather(lead_lower, "col", axis=1, tiled=True)
    reflect, left_root, inner_poly = transform_split(head_upper, head_lower, col_start, col_width)
    mixed_rows = upper_row - apply_transposed(reflect, lower_row)
    residue = lower_row - apply_rows(reflect, upper_row)
    pulled = apply_transposed(reflect, residue)
    upper_row = apply_rows(left_root, mixed_rows)
    lower_row = residue + apply_rows(reflect, apply_rows(inner_poly, pulled))
    return (upper_row, lower_row)


def solution(mesh):
    return jax.shard_map(
        shards,
        mesh=mesh,
        in_specs=(P(None, "blk", "col"), P(None, "blk", "col")),
        out_specs=(P(None, "blk", "col"), P(None, "blk", "col")),
        check_vma=False,
    )
```

profile of v0, /device:TPU:2, one launch (start us, length us, event | category | flops | bytes accessed | tf_op | source)
XLA Modules:
  0.0 550.1 jit_solution(15931930404348690198)
XLA Ops:
  7.2 0.0 all-reduce.3.cloned.1.call-start
  7.2 1.9 collective-permute-start
  9.1 0.7 broadcast_select_fusion
  9.9 5.2 collective-permute-done
  15.1 0.7 bitcast_select_fusion
  15.8 0.0 all-reduce.3.cloned.1.call-update
  15.9 0.0 all-gather.8.cloned.1.call-start
  15.9 341.9 %all-reduce.3.cloned.1.call-done = (f32[512,128]{1,0:T(8,128)}, f32[512,128]{1,0:T(8,128)}) async-done(((f32[512,128]{1,0:T(8,128)}, f32[512,128]{1,0:T(8,128)}), (f32[512,128]{1,0:T(8,128)}, f32[512,128]{1,0:T(8,128)})) %all-reduce.3.cloned.1.call-update) | async-done | bytes 524304 | tf_op jit(solution)/shard_map/psum | solution.py:17
  357.8 0.0 all-gather.8.cloned.1.call-update
  357.8 0.0 all-gather.6.cloned.1.call-start
  357.8 0.7 all-gather.6.cloned.1.call-update
  358.5 0.0 all-gather.10.cloned.1.call-start
  358.6 0.1 iota_compare_fusion
  358.7 31.3 %all-gather.8.cloned.1.call-done = f32[512,512]{1,0:T(8,128)} async-done(((f32[512,128]{1,0:T(8,128)}), f32[512,512]{1,0:T(8,128)}) %all-gather.8.cloned.1.call-update) | async-done | bytes 1048592 | tf_op jit(solution)/shard_map/all_gather | solution.py:89
  389.9 0.0 copy-start.1
  389.9 2.2 multiply_reduce_fusion
  392.8 0.0 copy-done.1
  392.8 0.2 subtract_divide_fusion
  393.0 1.0 convolution_subtract_fusion
  394.0 1.0 fusion.18
  395.0 31.2 %all-gather.6.cloned.1.call-done = f32[512,512]{1,0:T(8,128)} async-done(((f32[512,128]{1,0:T(8,128)}), f32[512,512]{1,0:T(8,128)}) %all-gather.6.cloned.1.call-update) | async-done | bytes 1048592 | tf_op jit(solution)/shard_map/all_gather | solution.py:90
  426.1 2.9 fusion.19
  429.1 0.0 all-gather.10.cloned.1.call-update
  429.1 0.0 all-gather.14.cloned.1.call-start
  429.1 34.2 %all-gather.10.cloned.1.call-done = f32[512,512]{1,0:T(8,128)} async-done(((f32[512,128]{1,0:T(8,128)}), f32[512,512]{1,0:T(8,128)}) %all-gather.10.cloned.1.call-update) | async-done | bytes 1048592 | tf_op jit(solution)/shard_map/all_gather | solution.py:59
  463.3 3.4 fusion.20
  466.7 1.0 fusion.14
  467.7 1.7 fusion.7
  469.4 0.0 all-gather.14.cloned.1.call-update
  469.5 0.2 all-gather.12.cloned.1.call-start
  469.7 0.0 copy-start
  469.7 1.7 fusion
  471.4 0.0 copy-start.2
  471.4 0.0 all-gather.12.cloned.1.call-update
  471.4 0.0 copy-done
  471.4 0.9 copy-done.2
  472.3 1.8 fusion.2
  474.2 1.0 fusion.3
  475.2 1.8 fusion.10
  477.0 26.7 %all-gather.14.cloned.1.call-done = f32[512,512]{1,0:T(8,128)} async-done(((f32[512,128]{1,0:T(8,128)}), f32[512,512]{1,0:T(8,128)}) %all-gather.14.cloned.1.call-update) | async-done | bytes 1048592 | tf_op jit(solution)/shard_map/all_gather | solution.py:75
  503.7 2.2 fusion.22
  505.9 1.7 fusion.4
  507.6 32.7 %all-gather.12.cloned.1.call-done = f32[512,512]{1,0:T(8,128)} async-done(((f32[512,128]{1,0:T(8,128)}), f32[512,512]{1,0:T(8,128)}) %all-gather.12.cloned.1.call-update) | async-done | bytes 1048592 | tf_op jit(solution)/shard_map/all_gather | solution.py:74
  540.3 2.9 fusion.21
Async XLA Ops:
  7.2 350.6 %all-reduce.3.cloned.1.call-start = ((), (), s32[]{:S(2)}) async-start(), calls=%async_computation.5 | async-start | bytes 1048576 | tf_op jit(solution)/shard_map/psum | solution.py:17
  7.2 7.9 %collective-permute-start = (f32[512,1,128]{2,0,1:T(8,128)}, f32[512,1,128]{2,0,1:T(8,128)S(1)}, u32[]{:S(2)}, u32[]{:S(2)}) collective-permute-start(f32[512,1,128]{2,0,1:T(8,128)} %bitcast.57), channel_id=1, source_target_pairs={{0,4},{4,8},{8,12},{12,16},{16,20},{20,24},{24,28},{28,32},{32,36}... | collective-permute-start | bytes 786440 | tf_op jit(solution)/shard_map/ppermute | solution.py:12
  15.9 374.1 %all-gather.8.cloned.1.call-start = ((), (), s32[]{:S(2)}) async-start(), calls=%async_computation.1 | async-start | bytes 1310720 | tf_op jit(solution)/shard_map/all_gather | solution.py:89
  357.8 68.4 %all-gather.6.cloned.1.call-start = ((), (), s32[]{:S(2)}) async-start(), calls=%async_computation | async-start | bytes 1310720 | tf_op jit(solution)/shard_map/all_gather | solution.py:90
  358.5 104.8 %all-gather.10.cloned.1.call-start = ((), (), s32[]{:S(2)}) async-start(), calls=%async_computation.2 | async-start | bytes 1310720 | tf_op jit(solution)/shard_map/all_gather | solution.py:59
  389.9 2.9 copy-start.1
  429.1 74.6 %all-gather.14.cloned.1.call-start = ((), (), s32[]{:S(2)}) async-start(), calls=%async_computation.4 | async-start | bytes 1310720 | tf_op jit(solution)/shard_map/all_gather | solution.py:75
  469.5 70.9 %all-gather.12.cloned.1.call-start = ((), (), s32[]{:S(2)}) async-start(), calls=%async_computation.3 | async-start | bytes 1310720 | tf_op jit(solution)/shard_map/all_gather | solution.py:74
  469.7 1.7 copy-start
  471.4 0.9 copy-start.2
Sparse Core Ops, SparseCore 0:
  16.0 341.7 all-reduce.2
  359.8 30.0 all-gather.7
  392.0 34.0 all-gather.5
  429.2 34.0 all-gather.9
  469.6 34.0 all-gather.13
  506.2 34.0 all-gather.11
where the time goes:
time: 550 us
  waiting for transfers between devices  504 us (92%)
  matrix products  24.1 us (4%)
  between operations  14.9 us (3%)
    psum x1, waiting for transfers between devices, broadcast(): return lax.psum(block, axis)  342 us
    all_gather x1, waiting for transfers between devices, transform_split(): reflect = lax.all_gather(reflect_part, 'col', axis=1, tiled=True)  34.2 us
    all_gather x1, waiting for transfers between devices, transform_split(): lax.all_gather(left_part, 'col', axis=1, tiled=True)  32.7 us
    all_gather x1, waiting for transfers between devices, shards(): head_upper = lax.all_gather(lead_upper, 'col', axis=1, tiled=True)  31.3 us
    all_gather x1, waiting for transfers between devices, shards(): head_lower = lax.all_gather(lead_lower, 'col', axis=1, tiled=True)  31.2 us
    all_gather x1, waiting for transfers between devices, transform_split(): lax.all_gather(inner_part, 'col', axis=1, tiled=True)  26.7 us
  transfers between devices with their start and end apart: 7, of which 7 were waited for; matrix products, arithmetic and copies ran while one was open for 3% of the time, Pallas kernels for 0%

commit v1 on v0

v1 whole, which is shorter than its diff:
```python
import jax
import jax.numpy as jnp
from jax import lax
from jax.experimental import pallas as pl
from jax.experimental.pallas import tpu as pltpu
from jax.sharding import PartitionSpec as P

MESH_ID = pl.DeviceIdType.MESH
F32 = jnp.float32
BF16 = jnp.bfloat16
B = 512
W = 128
Q = 128
NT = (((1,), (1,)), ((), ()))


def split(value):
    hi = value.astype(BF16)
    lo = (value - hi.astype(F32)).astype(BF16)
    return hi, lo


def left_form(value):
    hi, lo = split(value)
    return jnp.concatenate([hi, lo, hi], axis=1)


def dot_nn(left, right):
    return jnp.dot(left, right, preferred_element_type=F32)


def dot_nt(left, right):
    return lax.dot_general(left, right, NT, preferred_element_type=F32)


def communicate(u_in, l_in, buf, ush, loc, sems):
    blk = lax.axis_index("blk")
    y = lax.axis_index("col")
    z, x, c = blk // 8, (blk // 2) % 4, blk % 2
    a, b = x + c * (y - x), y + c * (x - y)
    rdy_in, rdy_out = sems["rdy_p"], sems["rdy_m"]
    odd = z % 2 == 1
    plus = z < 8

    def dev(zz, xx, yy, cc):
        return ((zz * 4 + xx) * 2 + cc, yy)

    def dev_ab(aa, bb):
        return dev(z, aa + c * (bb - aa), bb + c * (aa - bb), c)

    def region(aa, bb, start=0, rows=Q):
        yy, qq = bb + c * (aa - bb), aa + c * (bb - aa)
        return buf.at[c, yy, pl.ds(qq * Q + start, rows), :]

    pending = []

    def send(src, dst, send_sem, recv_sem, device):
        copy = pltpu.make_async_remote_copy(
            src_ref=src, dst_ref=dst, send_sem=send_sem, recv_sem=recv_sem,
            device_id=device, device_id_type=MESH_ID,
        )
        copy.start()
        return copy

    def arrived(dst, recv_sem):
        pltpu.make_async_copy(dst, dst, recv_sem).wait()

    bar = pltpu.get_barrier_semaphore()

    def hello(device):
        pl.semaphore_signal(bar, inc=1, device_id=device, device_id_type=MESH_ID)

    for d in (1, 2, 3):
        hello(dev_ab((a + d) % 4, b))
        hello(dev_ab(a, (b + d) % 4))
    hello(dev(z, x, y, 1 - c))
    gets_shift = jnp.logical_and(c == 0, blk > 0)
    sends_far = jnp.logical_and(c == 1, blk < 127)
    hub_relays = jnp.logical_and(odd, z != 9)

    @pl.when(gets_shift)
    def _():
        hello((blk - 1, y))

    @pl.when(z == 0)
    def _():
        hello(dev(1, x, y, c))
        hello(dev(15, x, y, c))

    @pl.when(jnp.logical_and(odd, z < 7))
    def _():
        hello(dev(z + 2, x, y, c))

    @pl.when(jnp.logical_and(odd, z > 9))
    def _():
        hello(dev(z - 2, x, y, c))

    even_far = jnp.logical_and(z % 2 == 0, z > 0)

    @pl.when(jnp.logical_and(even_far, z <= 8))
    def _():
        hello(dev(z - 1, x, y, c))

    @pl.when(jnp.logical_and(even_far, z > 8))
    def _():
        hello(dev(z + 1, x, y, c))

    local_l = pltpu.make_async_copy(l_in, loc, sems["loc"])
    local_l.start()
    pl.semaphore_wait(
        bar, 7 + sends_far.astype(jnp.int32) + odd.astype(jnp.int32) + hub_relays.astype(jnp.int32)
    )

    @pl.when(jnp.logical_and(odd, z < 8))
    def _():
        @pl.when(z < 7)
        def _():
            pl.semaphore_wait(sems["rdy_p"], 1)

        pl.semaphore_signal(
            sems["rdy_p"], inc=1, device_id=dev(jnp.maximum(z - 2, 0), x, y, c), device_id_type=MESH_ID
        )

    @pl.when(jnp.logical_and(odd, z > 8))
    def _():
        @pl.when(z > 9)
        def _():
            pl.semaphore_wait(sems["rdy_m"], 1)

        pl.semaphore_signal(
            sems["rdy_m"], inc=1, device_id=dev((z + 2 - (z // 15)) % 16, x, y, c), device_id_type=MESH_ID
        )

    shift = pltpu.make_async_remote_copy(
        src_ref=u_in, dst_ref=ush, send_sem=sems["sh_s"], recv_sem=sems["sh_r"],
        device_id=(jnp.minimum(blk + 1, 127), y), device_id_type=MESH_ID,
    )
    has_next = blk < 127

    @pl.when(jnp.logical_and(z > 0, has_next))
    def _():
        shift.start()

    own = region(a, b)
    root = jnp.logical_and(z == 0, x == 0)

    def scatter_from(src_ref):
        for d in (2, 1, 3):
            rows = pl.ds(d * Q, Q)
            send(src_ref.at[rows, :], buf.at[c, y, rows, :], sems["a_s"].at[d - 1], sems["own_r"],
                 dev(0, d, y, c))
        pltpu.make_async_copy(src_ref.at[pl.ds(0, Q), :], buf.at[c, y, pl.ds(0, Q), :], sems["own_r"]).start()

    @pl.when(jnp.logical_and(root, c == 0))
    def _():
        scatter_from(u_in)

    @pl.when(jnp.logical_and(root, c == 1))
    def _():
        scatter_from(l_in)

    arrived(own, sems["own_r"])

    @pl.when(z == 0)
    def _():
        pl.semaphore_wait(sems["rdy_p"], 1)
        pl.semaphore_wait(sems["rdy_m"], 1)
        for i, h in enumerate((7, 5, 3, 1)):
            send(own, own, sems["b_s"].at[i], sems["own_r"], dev(h, x, y, c))
            send(own, own, sems["b_s"].at[4 + i], sems["own_r"], dev(16 - h, x, y, c))

    @pl.when(hub_relays)
    def _():
        send(own, own, sems["b_s"].at[0], sems["own_r"], dev(z + 1 - 2 * (z // 8), x, y, c))

    def to_a(d):
        send(own, own, sems["c1_s"].at[d - 1], sems["c1_r"].at[d - 1], dev_ab((a + d) % 4, b))

    def to_b(j):
        piece = region((a + 4 - j) % 4, b)
        send(piece, piece, sems["fp_s"].at[j], sems["fp_r"].at[j], dev_ab(a, (b + 1) % 4))
        send(piece, piece, sems["fm_s"].at[j], sems["fm_r"].at[j], dev_ab(a, (b + 3) % 4))

    def to_partner(aa, bb, index):
        piece = region(aa, bb)
        send(piece, piece, sems["pt_s"].at[index], sems["pt_r"].at[index], dev(z, x, y, 1 - c))

    def relay(j):
        aj = (a + 4 - j) % 4
        arrived(region(aj, (b + 3) % 4), sems["fp_r"].at[j])
        half = region(aj, (b + 3) % 4, 0, Q // 2)
        send(half, half, sems["hp_s"].at[j], sems["hp_r"].at[j], dev_ab(a, (b + 1) % 4))
        arrived(region(aj, (b + 1) % 4), sems["fm_r"].at[j])
        half = region(aj, (b + 1) % 4, Q // 2, Q // 2)
        send(half, half, sems["hm_s"].at[j], sems["hm_r"].at[j], dev_ab(a, (b + 3) % 4))
        to_partner(aj, (b + 3) % 4, 4 + j)
        to_partner(aj, (b + 1) % 4, 8 + j)

    def took_a(d):
        arrived(region((a + 4 - d) % 4, b), sems["c1_r"].at[d - 1])
        to_b(d)
        to_partner((a + 4 - d) % 4, b, d)

    for d in (2, 1, 3):
        to_a(d)
    to_b(0)
    to_partner(a, b, 0)

    @pl.when(jnp.logical_and(z == 0, has_next))
    def _():
        shift.start()

    @pl.when(blk == 0)
    def _():
        ush[...] = jnp.zeros_like(ush)

    took_a(1)
    took_a(3)
    relay(0)
    took_a(2)
    for j in (1, 3, 2):
        relay(j)
    for j in (0, 1, 3, 2):
        aj, bb = (a + 4 - j) % 4, (b + 2) % 4
        arrived(region(aj, bb, 0, Q // 2), sems["hp_r"].at[j])
        arrived(region(aj, bb, Q // 2, Q // 2), sems["hm_r"].at[j])
        to_partner(aj, bb, 12 + j)

    local_l.wait()

    @pl.when(blk > 0)
    def _():
        arrived(ush, sems["sh_r"])

    e = 1 - c
    pa, pb = x + e * (y - x), y + e * (x - y)
    for index in range(16):
        j, s = index % 4, (0, 3, 1, 2)[index // 4]
        aa, bb = (pa + 4 - j) % 4, (pb + s) % 4
        yy, qq = bb + e * (aa - bb), aa + e * (bb - aa)
        arrived(buf.at[e, yy, pl.ds(qq * Q, Q), :], sems["pt_r"].at[index])

    def finish():
        def sent(ref, sem):
            pltpu.make_async_copy(ref, ref, sem).wait()

        full, half = region(0, 0), region(0, 0, 0, Q // 2)
        for j in range(4):
            sent(full, sems["fp_s"].at[j])
            sent(full, sems["fm_s"].at[j])
            sent(half, sems["hp_s"].at[j])
            sent(half, sems["hm_s"].at[j])
        for j in range(3):
            sent(full, sems["c1_s"].at[j])
        for j in range(16):
            sent(full, sems["pt_s"].at[j])

        @pl.when(root)
        def _():
            for j in range(3):
                sent(full, sems["a_s"].at[j])

        @pl.when(z == 0)
        def _():
            for j in range(8):
                sent(full, sems["b_s"].at[j])

        @pl.when(hub_relays)
        def _():
            sent(full, sems["b_s"].at[0])

        @pl.when(has_next)
        def _():
            sent(ush, sems["sh_s"])

    finish()


def compute(buf, ush, loc, u_out, l_out, n_l, n_r, g_l, h_f, h_l, m_r, k_l, k_n, k_t, d_r):
    rows = lax.broadcasted_iota(jnp.int32, (B, W), 0)
    cols = lax.broadcasted_iota(jnp.int32, (B, W), 1)
    total = jnp.zeros((1, 1), F32)
    for y in range(4):
        f = buf[0, y]
        total = total + jnp.sum(f * f, keepdims=True)
    scale = jnp.sqrt(total / B + 1e-06)
    inv = 1.0 / scale

    def put_left(ref, span, value_hi, value_lo, at):
        ref[span, pl.ds(at, W)] = value_hi
        ref[span, pl.ds(B + at, W)] = value_lo
        ref[span, pl.ds(2 * B + at, W)] = value_hi

    whole = pl.ds(0, B)
    for y in range(4):
        at = y * W
        n = jnp.where(rows == cols + at, 1.0, 0.0) - buf[0, y] * inv
        hi, lo = split(n)
        put_left(n_l, whole, hi, lo, at)
        n_r[pl.ds(0, B), pl.ds(at, W)] = hi
        n_r[pl.ds(B, B), pl.ds(at, W)] = hi
        n_r[pl.ds(2 * B, B), pl.ds(at, W)] = lo
        hi, lo = split(buf[1, y])
        put_left(g_l, whole, hi, lo, at)

    step = 256

    def first(i, carry):
        at = pl.multiple_of(i * step, step)
        span = pl.ds(at, step)
        g = jnp.concatenate([buf[1, y, span, :] for y in range(4)], axis=1)
        h = g + dot_nn(g_l[span, :], n_r[...])
        h_f[span, :] = h
        h_l[span, :] = left_form(h)
        hi, lo = split(dot_nn(n_l[span, :], n_r[...]))
        m_r[span, :] = hi
        m_r[pl.ds(B + at, step), :] = hi
        m_r[pl.ds(2 * B + at, step), :] = lo
        return carry

    lax.fori_loop(0, B // step, first, 0)

    def second(i, carry):
        at = pl.multiple_of(i * step, step)
        span = pl.ds(at, step)
        k = (h_f[span, :] + dot_nn(h_l[span, :], m_r[...])) * inv
        hi, lo = split(k)
        k_n[span, :] = hi
        k_n[pl.ds(B + at, step), :] = hi
        k_n[pl.ds(2 * B + at, step), :] = lo
        k_l[span, :] = jnp.concatenate([hi, lo, hi], axis=1)
        k_t[span, :] = jnp.concatenate([hi, hi, lo], axis=1)
        return carry

    lax.fori_loop(0, B // step, second, 0)

    def third(i, carry):
        at = pl.multiple_of(i * step, step)
        span = pl.ds(at, step)
        hi, lo = split(dot_nt(k_l[span, :], k_t[...]))
        d_r[span, :] = hi
        d_r[pl.ds(B + at, step), :] = hi
        d_r[pl.ds(2 * B + at, step), :] = lo
        return carry

    lax.fori_loop(0, B // step, third, 0)

    low = loc[...].T
    up = ush[...].T
    mixed = up - dot_nn(left_form(low), k_n[...])
    rest = low - dot_nt(left_form(up), k_t[...])
    pulled = dot_nt(left_form(mixed), k_t[...])
    both = jnp.concatenate([rest, pulled], axis=0)
    part = 0.3125 * both + 0.0625 * dot_nn(left_form(both), d_r[...])
    part = 0.375 * both + dot_nn(left_form(part), d_r[...])
    part = 0.5 * both + dot_nn(left_form(part), d_r[...])
    u_out[...] = (mixed + dot_nn(left_form(part[W:]), k_n[...])).T
    l_out[...] = (rest + dot_nn(left_form(part[:W]), d_r[...])).T


SEMS = {
    "rdy_p": None, "rdy_m": None, "loc": (), "sh_s": (), "sh_r": (), "own_r": (),
    "a_s": (3,), "b_s": (8,), "c1_s": (3,), "c1_r": (3,),
    "fp_s": (4,), "fp_r": (4,), "fm_s": (4,), "fm_r": (4,),
    "hp_s": (4,), "hp_r": (4,), "hm_s": (4,), "hm_r": (4,),
    "pt_s": (16,), "pt_r": (16,),
}


def kernel(u_in, l_in, u_out, l_out, buf, ush, loc, *rest):
    mats, sems = rest[:10], dict(zip(SEMS, rest[10:]))
    communicate(u_in, l_in, buf, ush, loc, sems)
    compute(buf, ush, loc, u_out, l_out, *mats)


def shards(upper_row, lower_row):
    shape = jax.ShapeDtypeStruct((B, W), F32)
    cat_l, cat_r = pltpu.VMEM((B, 3 * B), BF16), pltpu.VMEM((3 * B, B), BF16)
    sems = [
        pltpu.SemaphoreType.REGULAR if s is None else pltpu.SemaphoreType.DMA(s) for s in SEMS.values()
    ]
    new_upper, new_lower = pl.pallas_call(
        kernel,
        out_shape=(shape, shape),
        in_specs=[pl.BlockSpec(memory_space=pl.ANY)] * 2,
        out_specs=[pl.BlockSpec(memory_space=pltpu.VMEM)] * 2,
        scratch_shapes=[
            pltpu.VMEM((2, 4, B, W), F32), pltpu.VMEM((B, W), F32), pltpu.VMEM((B, W), F32),
            cat_l, cat_r, cat_l, pltpu.VMEM((B, B), F32), cat_l, cat_r, cat_l, cat_r, cat_l, cat_r,
            *sems,
        ],
        compiler_params=pltpu.CompilerParams(
            collective_id=0, has_side_effects=True, vmem_limit_bytes=56 * 1024 * 1024
        ),
        name="schur",
    )(upper_row.reshape(B, W), lower_row.reshape(B, W))
    return new_upper.reshape(B, 1, W), new_lower.reshape(B, 1, W)


def solution(mesh):
    spec = P(None, "blk", "col")
    return jax.shard_map(
        shards, mesh=mesh, in_specs=(spec, spec), out_specs=(spec, spec), check_vma=False
    )
```

time: 550 us -> 58 us (0.11)
  the two profiles are of different devices: /device:TPU:2 before, /device:TPU:65 now
where the time goes in v1:
time: 58 us; the launch traced here: 57.8 us
  Pallas kernels  54.7 us (94%)
  local copies, waits for them, and re-layouts  2.42 us (4%)
  between operations  0.65 us (1%)
    pallas_call x1, Pallas kernels, shards(): pl.pallas_call(kernel, out_shape=(shape, shape), in_specs=[pl.BlockSpec(m...  54.7 us
    unnamed x4, local copies, waits for them, and re-layouts  2.42 us

profile of v1, /device:TPU:65, one launch (start us, length us, event | category | flops | bytes accessed | tf_op | source)
XLA Modules:
  0.0 57.8 jit_solution(9840638256061943441)
XLA Ops:
  0.6 54.7 %schur.1 = (f32[512,128]{1,0:T(8,128)}, f32[512,128]{1,0:T(8,128)}) custom-call(f32[512,128]{1,0:T(8,128)} %bitcast.8, f32[512,128]{1,0:T(8,128)} %bitcast.9), custom_call_target="tpu_custom_call" | custom-call | tf_op jit(solution)/shard_map/schur/pallas_call | solution.py:382
  55.4 0.0 copy-start
  55.4 1.7 %copy.8 = f32[512,1,128]{2,1,0:T(1,128)} copy(f32[512,1,128]{2,1,0:T(1,128)} %bitcast.11) | data formatting | bytes 524288
  57.1 0.0 copy-done
  57.1 0.7 %copy.9 = f32[512,1,128]{2,1,0:T(1,128)} copy(f32[512,1,128]{2,1,0:T(1,128)S(1)} %bitcast.10) | data formatting | bytes 524288
Async XLA Ops:
  55.4 1.7 %copy-start = (f32[512,128]{1,0:T(8,128)S(1)}, f32[512,128]{1,0:T(8,128)}, u32[]{:S(2)}) copy-start(f32[512,128]{1,0:T(8,128)} %get-tuple-element.5) | copy-start | bytes 786436

commit v2 on v1

--- a/solution.py
+++ b/solution.py
@@ -38,7 +38,6 @@
     y = lax.axis_index("col")
     z, x, c = blk // 8, (blk // 2) % 4, blk % 2
     a, b = x + c * (y - x), y + c * (x - y)
-    rdy_in, rdy_out = sems["rdy_p"], sems["rdy_m"]
     odd = z % 2 == 1
     plus = z < 8
 
@@ -66,80 +65,79 @@
         pltpu.make_async_copy(dst, dst, recv_sem).wait()
 
     bar = pltpu.get_barrier_semaphore()
-
-    def hello(device):
-        pl.semaphore_signal(bar, inc=1, device_id=device, device_id_type=MESH_ID)
-
-    for d in (1, 2, 3):
-        hello(dev_ab((a + d) % 4, b))
-        hello(dev_ab(a, (b + d) % 4))
-    hello(dev(z, x, y, 1 - c))
-    gets_shift = jnp.logical_and(c == 0, blk > 0)
+    first = jnp.logical_and(blk == 0, y == 0)
+    proxy = jnp.logical_and(blk == 1, y == 0)
+    column = jnp.logical_and(x == 0, y == 0)
+    head = jnp.logical_and(z == 0, jnp.logical_not(first))
+    near_row = jnp.logical_and(c == 0, (x == 0) != (y == 0))
+    near = jnp.logical_and(z == 0, jnp.logical_or(near_row, jnp.logical_and(c == 1, column)))
+    gets_far = jnp.logical_and(c == 0, blk > 0)
     sends_far = jnp.logical_and(c == 1, blk < 127)
-    hub_relays = jnp.logical_and(odd, z != 9)
-
-    @pl.when(gets_shift)
-    def _():
-        hello((blk - 1, y))
-
-    @pl.when(z == 0)
-    def _():
-        hello(dev(1, x, y, c))
-        hello(dev(15, x, y, c))
-
-    @pl.when(jnp.logical_and(odd, z < 7))
-    def _():
-        hello(dev(z + 2, x, y, c))
-
-    @pl.when(jnp.logical_and(odd, z > 9))
-    def _():
-        hello(dev(z - 2, x, y, c))
-
+    has_next = blk < 127
+    relays = jnp.logical_and(odd, z != 9)
+    relay_z = z + 1 - 2 * (z // 8)
     even_far = jnp.logical_and(z % 2 == 0, z > 0)
-
-    @pl.when(jnp.logical_and(even_far, z <= 8))
-    def _():
-        hello(dev(z - 1, x, y, c))
-
-    @pl.when(jnp.logical_and(even_far, z > 8))
-    def _():
-        hello(dev(z + 1, x, y, c))
+    inner_z = z - 1 + 2 * ((z - 1) // 8)
+
+    def signal(sem, device):
+        pl.semaphore_signal(sem, inc=1, device_id=device, device_id_type=MESH_ID)
+
+    def each_peer(act):
+        for d in (1, 2, 3):
+            act(dev_ab((a + d) % 4, b))
+            act(dev_ab(a, (b + d) % 4))
+        act(dev(z, x, y, 1 - c))
+
+    @pl.when(jnp.logical_not(first))
+    def _():
+        each_peer(lambda device: signal(bar, device))
+
+    @pl.when(sends_far)
+    def _():
+        signal(bar, (blk + 1, y))
+
+    @pl.when(head)
+    def _():
+        for h in HUBS:
+            signal(bar, dev(h, x, y, c))
+
+    @pl.when(proxy)
+    def _():
+        for h in HUBS:
+            signal(bar, dev(h, x, y, 0))
+
+    @pl.when(relays)
+    def _():
+        signal(bar, dev(relay_z, x, y, c))
 
     local_l = pltpu.make_async_copy(l_in, loc, sems["loc"])
     local_l.start()
     pl.semaphore_wait(
-        bar, 7 + sends_far.astype(jnp.int32) + odd.astype(jnp.int32) + hub_relays.astype(jnp.int32)
+        bar, 7 - near.astype(jnp.int32) + gets_far.astype(jnp.int32) + (z > 0).astype(jnp.int32)
     )
 
-    @pl.when(jnp.logical_and(odd, z < 8))
-    def _():
-        @pl.when(z < 7)
-        def _():
-            pl.semaphore_wait(sems["rdy_p"], 1)
-
-        pl.semaphore_signal(
-            sems["rdy_p"], inc=1, device_id=dev(jnp.maximum(z - 2, 0), x, y, c), device_id_type=MESH_ID
-        )
-
-    @pl.when(jnp.logical_and(odd, z > 8))
-    def _():
-        @pl.when(z > 9)
-        def _():
-            pl.semaphore_wait(sems["rdy_m"], 1)
-
-        pl.semaphore_signal(
-            sems["rdy_m"], inc=1, device_id=dev((z + 2 - (z // 15)) % 16, x, y, c), device_id_type=MESH_ID
-        )
+    @pl.when(first)
+    def _():
+        each_peer(lambda device: signal(sems["late"], device))
+
+    @pl.when(odd)
+    def _():
+        lone = jnp.logical_and(column, c == 0).astype(jnp.int32)
+        index = jnp.where(plus, z // 2, 4 + (15 - z) // 2) + 8 * lone
+        signal(sems["crd"].at[index], dev(0, x, y, c + lone))
+
+    @pl.when(even_far)
+    def _():
+        signal(sems["rc"], dev(inner_z, x, y, c))
+
+    @pl.when(gets_far)
+    def _():
+        signal(sems["sh_c"], (blk - 1, y))
 
     shift = pltpu.make_async_remote_copy(
         src_ref=u_in, dst_ref=ush, send_sem=sems["sh_s"], recv_sem=sems["sh_r"],
         device_id=(jnp.minimum(blk + 1, 127), y), device_id_type=MESH_ID,
     )
-    has_next = blk < 127
-
-    @pl.when(jnp.logical_and(z > 0, has_next))
-    def _():
-        shift.start()
 
     own = region(a, b)
     root = jnp.logical_and(z == 0, x == 0)
@@ -161,17 +159,28 @@
 
     arrived(own, sems["own_r"])
 
-    @pl.when(z == 0)
-    def _():
-        pl.semaphore_wait(sems["rdy_p"], 1)
-        pl.semaphore_wait(sems["rdy_m"], 1)
-        for i, h in enumerate((7, 5, 3, 1)):
-            send(own, own, sems["b_s"].at[i], sems["own_r"], dev(h, x, y, c))
-            send(own, own, sems["b_s"].at[4 + i], sems["own_r"], dev(16 - h, x, y, c))
-
-    @pl.when(hub_relays)
-    def _():
-        send(own, own, sems["b_s"].at[0], sems["own_r"], dev(z + 1 - 2 * (z // 8), x, y, c))
+    lone_piece = buf.at[0, 0, pl.ds(0, Q), :]
+
+    def to_hubs(piece, core, base, picks):
+        for i in picks:
+            pl.semaphore_wait(sems["crd"].at[base + i], 1)
+            send(piece, piece, sems["b_s"].at[base + i], sems["own_r"], dev(HUBS[i], x, y, core))
+
+    @pl.when(head)
+    def _():
+        for n, picks in enumerate(((0, 1, 2), (4, 5, 6), (3, 7))):
+            to_hubs(own, c, 0, picks)
+
+            @pl.when(proxy)
+            def _():
+                if n == 0:
+                    arrived(lone_piece, sems["pt_r"].at[0])
+                to_hubs(lone_piece, 0, 8, picks)
+
+    @pl.when(relays)
+    def _():
+        pl.semaphore_wait(sems["rc"], 1)
+        send(own, own, sems["b_s"].at[0], sems["own_r"], dev(relay_z, x, y, c))
 
     def to_a(d):
         send(own, own, sems["c1_s"].at[d - 1], sems["c1_r"].at[d - 1], dev_ab((a + d) % 4, b))
@@ -201,12 +210,20 @@
         to_b(d)
         to_partner((a + 4 - d) % 4, b, d)
 
+    @pl.when(near)
+    def _():
+        pl.semaphore_wait(sems["late"], 1)
+
+    to_partner(a, b, 0)
     for d in (2, 1, 3):
         to_a(d)
     to_b(0)
-    to_partner(a, b, 0)
-
-    @pl.when(jnp.logical_and(z == 0, has_next))
+
+    @pl.when(sends_far)
+    def _():
+        pl.semaphore_wait(sems["sh_c"], 1)
+
+    @pl.when(has_next)
     def _():
         shift.start()
 
@@ -238,7 +255,14 @@
         j, s = index % 4, (0, 3, 1, 2)[index // 4]
         aa, bb = (pa + 4 - j) % 4, (pb + s) % 4
         yy, qq = bb + e * (aa - bb), aa + e * (bb - aa)
-        arrived(buf.at[e, yy, pl.ds(qq * Q, Q), :], sems["pt_r"].at[index])
+        piece = buf.at[e, yy, pl.ds(qq * Q, Q), :]
+        if index == 0:
+
+            @pl.when(jnp.logical_not(proxy))
+            def _():
+                arrived(piece, sems["pt_r"].at[index])
+        else:
+            arrived(piece, sems["pt_r"].at[index])
 
     def finish():
         def sent(ref, sem):
@@ -260,12 +284,17 @@
             for j in range(3):
                 sent(full, sems["a_s"].at[j])
 
-        @pl.when(z == 0)
+        @pl.when(head)
         def _():
             for j in range(8):
                 sent(full, sems["b_s"].at[j])
 
-        @pl.when(hub_relays)
+        @pl.when(proxy)
+        def _():
+            for j in range(8, 16):
+                sent(full, sems["b_s"].at[j])
+
+        @pl.when(relays)
         def _():
             sent(full, sems["b_s"].at[0])
 
@@ -358,9 +387,11 @@
     l_out[...] = (rest + dot_nn(left_form(part[:W]), d_r[...])).T
 
 
+REG, REG16 = "one", "many"
+HUBS = (1, 3, 5, 7, 15, 13, 11, 9)
 SEMS = {
-    "rdy_p": None, "rdy_m": None, "loc": (), "sh_s": (), "sh_r": (), "own_r": (),
-    "a_s": (3,), "b_s": (8,), "c1_s": (3,), "c1_r": (3,),
+    "late": REG, "rc": REG, "sh_c": REG, "crd": REG16, "loc": (), "sh_s": (), "sh_r": (), "own_r": (),
+    "a_s": (3,), "b_s": (16,), "c1_s": (3,), "c1_r": (3,),
     "fp_s": (4,), "fp_r": (4,), "fm_s": (4,), "fm_r": (4,),
     "hp_s": (4,), "hp_r": (4,), "hm_s": (4,), "hm_r": (4,),
     "pt_s": (16,), "pt_r": (16,),
@@ -376,9 +407,8 @@
 def shards(upper_row, lower_row):
     shape = jax.ShapeDtypeStruct((B, W), F32)
     cat_l, cat_r = pltpu.VMEM((B, 3 * B), BF16), pltpu.VMEM((3 * B, B), BF16)
-    sems = [
-        pltpu.SemaphoreType.REGULAR if s is None else pltpu.SemaphoreType.DMA(s) for s in SEMS.values()
-    ]
+    kinds = {REG: pltpu.SemaphoreType.REGULAR, REG16: pltpu.SemaphoreType.REGULAR((16,))}
+    sems = [kinds[s] if s in kinds else pltpu.SemaphoreType.DMA(s) for s in SEMS.values()]
     new_upper, new_lower = pl.pallas_call(
         kernel,
         out_shape=(shape, shape),

time: 58 us -> 49.5 us (0.85)
  the two profiles are of different devices: /device:TPU:65 before, /device:TPU:257 now
where the time goes in v2:
time: 49.5 us; the launch traced here: 49.4 us
  Pallas kernels  46.3 us (94%)
  local copies, waits for them, and re-layouts  2.42 us (5%)
  between operations  0.65 us (1%)
    pallas_call x1, Pallas kernels, shards(): pl.pallas_call(kernel, out_shape=(shape, shape), in_specs=[pl.BlockSpec(m...  46.3 us
    unnamed x4, local copies, waits for them, and re-layouts  2.42 us

profile of v2, /device:TPU:257, one launch (start us, length us, event | category | flops | bytes accessed | tf_op | source)
XLA Modules:
  0.0 49.4 jit_solution(17841037074710079263)
XLA Ops:
  0.6 46.3 %schur.1 = (f32[512,128]{1,0:T(8,128)}, f32[512,128]{1,0:T(8,128)}) custom-call(f32[512,128]{1,0:T(8,128)} %bitcast.8, f32[512,128]{1,0:T(8,128)} %bitcast.9), custom_call_target="tpu_custom_call" | custom-call | tf_op jit(solution)/shard_map/schur/pallas_call | solution.py:412
  46.9 0.0 copy-start
  47.0 1.7 %copy.8 = f32[512,1,128]{2,1,0:T(1,128)} copy(f32[512,1,128]{2,1,0:T(1,128)} %bitcast.11) | data formatting | bytes 524288
  48.7 0.0 copy-done
  48.7 0.7 %copy.9 = f32[512,1,128]{2,1,0:T(1,128)} copy(f32[512,1,128]{2,1,0:T(1,128)S(1)} %bitcast.10) | data formatting | bytes 524288
Async XLA Ops:
  46.9 1.7 %copy-start = (f32[512,128]{1,0:T(8,128)S(1)}, f32[512,128]{1,0:T(8,128)}, u32[]{:S(2)}) copy-start(f32[512,128]{1,0:T(8,128)} %get-tuple-element.5) | copy-start | bytes 786436

commit v3 on v2

--- a/solution.py
+++ b/solution.py
@@ -38,8 +38,6 @@
     y = lax.axis_index("col")
     z, x, c = blk // 8, (blk // 2) % 4, blk % 2
     a, b = x + c * (y - x), y + c * (x - y)
-    odd = z % 2 == 1
-    plus = z < 8
 
     def dev(zz, xx, yy, cc):
         return ((zz * 4 + xx) * 2 + cc, yy)
@@ -74,10 +72,15 @@
     gets_far = jnp.logical_and(c == 0, blk > 0)
     sends_far = jnp.logical_and(c == 1, blk < 127)
     has_next = blk < 127
-    relays = jnp.logical_and(odd, z != 9)
-    relay_z = z + 1 - 2 * (z // 8)
-    even_far = jnp.logical_and(z % 2 == 0, z > 0)
-    inner_z = z - 1 + 2 * ((z - 1) // 8)
+    up = z <= 8
+    sign = 1 - 2 * (z // 9)
+    dist = jnp.where(up, z, 16 - z)
+    far2 = jnp.logical_or(dist == 4, z == 6)
+    far1 = jnp.logical_or(jnp.logical_or(dist == 2, dist == 4), z == 6)
+    far3 = z == 12
+    step_in = jnp.where(z == 9, 3, jnp.where(dist % 2 == 1, 1, jnp.where(dist == 4, 4, 2)))
+    parent = (z - sign * step_in + 16) % 16
+    slot = jnp.where(step_in >= 3, 0, jnp.where(step_in == 2, 1, 2)) + 3 * (z // 9)
 
     def signal(sem, device):
         pl.semaphore_signal(sem, inc=1, device_id=device, device_id_type=MESH_ID)
@@ -106,9 +109,17 @@
         for h in HUBS:
             signal(bar, dev(h, x, y, 0))
 
-    @pl.when(relays)
-    def _():
-        signal(bar, dev(relay_z, x, y, c))
+    @pl.when(far3)
+    def _():
+        signal(bar, dev(9, x, y, c))
+
+    @pl.when(far2)
+    def _():
+        signal(bar, dev(z + 2 * sign, x, y, c))
+
+    @pl.when(far1)
+    def _():
+        signal(bar, dev(z + sign, x, y, c))
 
     local_l = pltpu.make_async_copy(l_in, loc, sems["loc"])
     local_l.start()
@@ -120,15 +131,10 @@
     def _():
         each_peer(lambda device: signal(sems["late"], device))
 
-    @pl.when(odd)
-    def _():
-        lone = jnp.logical_and(column, c == 0).astype(jnp.int32)
-        index = jnp.where(plus, z // 2, 4 + (15 - z) // 2) + 8 * lone
-        signal(sems["crd"].at[index], dev(0, x, y, c + lone))
-
-    @pl.when(even_far)
-    def _():
-        signal(sems["rc"], dev(inner_z, x, y, c))
+    @pl.when(z > 0)
+    def _():
+        lone = jnp.logical_and(jnp.logical_and(column, c == 0), parent == 0).astype(jnp.int32)
+        signal(sems["crd"].at[slot + 6 * lone], dev(parent, x, y, c + lone))
 
     @pl.when(gets_far)
     def _():
@@ -138,6 +144,19 @@
         src_ref=u_in, dst_ref=ush, send_sem=sems["sh_s"], recv_sem=sems["sh_r"],
         device_id=(jnp.minimum(blk + 1, 127), y), device_id_type=MESH_ID,
     )
+
+    def start_shift():
+        @pl.when(sends_far)
+        def _():
+            pl.semaphore_wait(sems["sh_c"], 1)
+
+        @pl.when(has_next)
+        def _():
+            shift.start()
+
+    @pl.when(z > 0)
+    def _():
+        start_shift()
 
     own = region(a, b)
     root = jnp.logical_and(z == 0, x == 0)
@@ -161,32 +180,47 @@
 
     lone_piece = buf.at[0, 0, pl.ds(0, Q), :]
 
-    def to_hubs(piece, core, base, picks):
+    def to_child(piece, core, base, i, child):
+        pl.semaphore_wait(sems["crd"].at[base + i], 1)
+        send(piece, piece, sems["b_s"].at[base + i], sems["own_r"], dev(child, x, y, core))
+
+    def from_root(picks):
         for i in picks:
-            pl.semaphore_wait(sems["crd"].at[base + i], 1)
-            send(piece, piece, sems["b_s"].at[base + i], sems["own_r"], dev(HUBS[i], x, y, core))
+            to_child(own, c, 0, i, HUBS[i])
+
+    def from_proxy(picks):
+        for i in picks:
+            to_child(lone_piece, 0, 6, i, HUBS[i])
 
     @pl.when(head)
     def _():
-        for n, picks in enumerate(((0, 1, 2), (4, 5, 6), (3, 7))):
-            to_hubs(own, c, 0, picks)
-
-            @pl.when(proxy)
-            def _():
-                if n == 0:
-                    arrived(lone_piece, sems["pt_r"].at[0])
-                to_hubs(lone_piece, 0, 8, picks)
-
-    @pl.when(relays)
-    def _():
-        pl.semaphore_wait(sems["rc"], 1)
-        send(own, own, sems["b_s"].at[0], sems["own_r"], dev(relay_z, x, y, c))
+        from_root((0, 1, 2))
+
+    @pl.when(proxy)
+    def _():
+        arrived(lone_piece, sems["pt_r"].at[0])
+        from_proxy((0, 1, 2))
+
+    side = 3 * (z // 9)
+
+    @pl.when(far3)
+    def _():
+        to_child(own, c, 0, 3, 9)
+
+    @pl.when(far2)
+    def _():
+        to_child(own, c, 0, 1 + side, z + 2 * sign)
+
+    @pl.when(far1)
+    def _():
+        to_child(own, c, 0, 2 + side, z + sign)
 
     def to_a(d):
         send(own, own, sems["c1_s"].at[d - 1], sems["c1_r"].at[d - 1], dev_ab((a + d) % 4, b))
 
     def to_b(j):
         piece = region((a + 4 - j) % 4, b)
+        send(piece, piece, sems["hp_s"].at[j], sems["hp_r"].at[j], dev_ab(a, (b + 2) % 4))
         send(piece, piece, sems["fp_s"].at[j], sems["fp_r"].at[j], dev_ab(a, (b + 1) % 4))
         send(piece, piece, sems["fm_s"].at[j], sems["fm_r"].at[j], dev_ab(a, (b + 3) % 4))
 
@@ -194,16 +228,10 @@
         piece = region(aa, bb)
         send(piece, piece, sems["pt_s"].at[index], sems["pt_r"].at[index], dev(z, x, y, 1 - c))
 
-    def relay(j):
-        aj = (a + 4 - j) % 4
-        arrived(region(aj, (b + 3) % 4), sems["fp_r"].at[j])
-        half = region(aj, (b + 3) % 4, 0, Q // 2)
-        send(half, half, sems["hp_s"].at[j], sems["hp_r"].at[j], dev_ab(a, (b + 1) % 4))
-        arrived(region(aj, (b + 1) % 4), sems["fm_r"].at[j])
-        half = region(aj, (b + 1) % 4, Q // 2, Q // 2)
-        send(half, half, sems["hm_s"].at[j], sems["hm_r"].at[j], dev_ab(a, (b + 3) % 4))
-        to_partner(aj, (b + 3) % 4, 4 + j)
-        to_partner(aj, (b + 1) % 4, 8 + j)
+    def took_b(j, d, name):
+        aj, bd = (a + 4 - j) % 4, (b + 4 - d) % 4
+        arrived(region(aj, bd), sems[name].at[j])
+        to_partner(aj, bd, 4 * d + j)
 
     def took_a(d):
         arrived(region((a + 4 - d) % 4, b), sems["c1_r"].at[d - 1])
@@ -219,29 +247,28 @@
         to_a(d)
     to_b(0)
 
-    @pl.when(sends_far)
-    def _():
-        pl.semaphore_wait(sems["sh_c"], 1)
-
-    @pl.when(has_next)
-    def _():
-        shift.start()
+    @pl.when(head)
+    def _():
+        from_root((3, 4, 5))
+
+    @pl.when(proxy)
+    def _():
+        from_proxy((3, 4, 5))
+
+    @pl.when(z == 0)
+    def _():
+        start_shift()
 
     @pl.when(blk == 0)
     def _():
         ush[...] = jnp.zeros_like(ush)
 
-    took_a(1)
-    took_a(3)
-    relay(0)
-    took_a(2)
-    for j in (1, 3, 2):
-        relay(j)
-    for j in (0, 1, 3, 2):
-        aj, bb = (a + 4 - j) % 4, (b + 2) % 4
-        arrived(region(aj, bb, 0, Q // 2), sems["hp_r"].at[j])
-        arrived(region(aj, bb, Q // 2, Q // 2), sems["hm_r"].at[j])
-        to_partner(aj, bb, 12 + j)
+    for d in (3, 1, 2):
+        took_a(d)
+    for j in (0, 3, 1, 2):
+        took_b(j, 1, "fp_r")
+        took_b(j, 3, "fm_r")
+        took_b(j, 2, "hp_r")
 
     local_l.wait()
 
@@ -252,8 +279,8 @@
     e = 1 - c
     pa, pb = x + e * (y - x), y + e * (x - y)
     for index in range(16):
-        j, s = index % 4, (0, 3, 1, 2)[index // 4]
-        aa, bb = (pa + 4 - j) % 4, (pb + s) % 4
+        j, d = index % 4, index // 4
+        aa, bb = (pa + 4 - j) % 4, (pb + 4 - d) % 4
         yy, qq = bb + e * (aa - bb), aa + e * (bb - aa)
         piece = buf.at[e, yy, pl.ds(qq * Q, Q), :]
         if index == 0:
@@ -268,12 +295,11 @@
         def sent(ref, sem):
             pltpu.make_async_copy(ref, ref, sem).wait()
 
-        full, half = region(0, 0), region(0, 0, 0, Q // 2)
+        full = region(0, 0)
         for j in range(4):
             sent(full, sems["fp_s"].at[j])
             sent(full, sems["fm_s"].at[j])
-            sent(half, sems["hp_s"].at[j])
-            sent(half, sems["hm_s"].at[j])
+            sent(full, sems["hp_s"].at[j])
         for j in range(3):
             sent(full, sems["c1_s"].at[j])
         for j in range(16):
@@ -286,17 +312,25 @@
 
         @pl.when(head)
         def _():
-            for j in range(8):
+            for j in range(6):
                 sent(full, sems["b_s"].at[j])
 
         @pl.when(proxy)
         def _():
-            for j in range(8, 16):
+            for j in range(6, 12):
                 sent(full, sems["b_s"].at[j])
 
-        @pl.when(relays)
-        def _():
-            sent(full, sems["b_s"].at[0])
+        @pl.when(far3)
+        def _():
+            sent(full, sems["b_s"].at[3])
+
+        @pl.when(far2)
+        def _():
+            sent(full, sems["b_s"].at[1 + side])
+
+        @pl.when(far1)
+        def _():
+            sent(full, sems["b_s"].at[2 + side])
 
         @pl.when(has_next)
         def _():
@@ -388,12 +422,12 @@
 
 
 REG, REG16 = "one", "many"
-HUBS = (1, 3, 5, 7, 15, 13, 11, 9)
+HUBS = (4, 2, 1, 12, 14, 15)
 SEMS = {
-    "late": REG, "rc": REG, "sh_c": REG, "crd": REG16, "loc": (), "sh_s": (), "sh_r": (), "own_r": (),
-    "a_s": (3,), "b_s": (16,), "c1_s": (3,), "c1_r": (3,),
+    "late": REG, "sh_c": REG, "crd": REG16, "loc": (), "sh_s": (), "sh_r": (), "own_r": (),
+    "a_s": (3,), "b_s": (12,), "c1_s": (3,), "c1_r": (3,),
     "fp_s": (4,), "fp_r": (4,), "fm_s": (4,), "fm_r": (4,),
-    "hp_s": (4,), "hp_r": (4,), "hm_s": (4,), "hm_r": (4,),
+    "hp_s": (4,), "hp_r": (4,),
     "pt_s": (16,), "pt_r": (16,),
 }
 

time: 49.5 us -> 47.2 us (0.954)
  the two profiles are of different devices: /device:TPU:257 before, /device:TPU:225 now
where the time goes in v3:
time: 47.2 us; the launch traced here: 47 us
  Pallas kernels  44 us (93%)
  local copies, waits for them, and re-layouts  2.42 us (5%)
  between operations  0.65 us (1%)
    pallas_call x1, Pallas kernels, shards(): pl.pallas_call(kernel, out_shape=(shape, shape), in_specs=[pl.BlockSpec(m...  44 us
    unnamed x4, local copies, waits for them, and re-layouts  2.42 us

profile of v3, /device:TPU:225, one launch (start us, length us, event | category | flops | bytes accessed | tf_op | source)
XLA Modules:
  0.0 47.0 jit_solution(8132952150329928165)
XLA Ops:
  0.6 44.0 %schur.1 = (f32[512,128]{1,0:T(8,128)}, f32[512,128]{1,0:T(8,128)}) custom-call(f32[512,128]{1,0:T(8,128)} %bitcast.8, f32[512,128]{1,0:T(8,128)} %bitcast.9), custom_call_target="tpu_custom_call" | custom-call | tf_op jit(solution)/shard_map/schur/pallas_call | solution.py:446
  44.6 0.0 copy-start
  44.6 1.7 %copy.8 = f32[512,1,128]{2,1,0:T(1,128)} copy(f32[512,1,128]{2,1,0:T(1,128)} %bitcast.11) | data formatting | bytes 524288
  46.3 0.0 copy-done
  46.3 0.7 %copy.9 = f32[512,1,128]{2,1,0:T(1,128)} copy(f32[512,1,128]{2,1,0:T(1,128)S(1)} %bitcast.10) | data formatting | bytes 524288
Async XLA Ops:
  44.6 1.7 %copy-start = (f32[512,128]{1,0:T(8,128)S(1)}, f32[512,128]{1,0:T(8,128)}, u32[]{:S(2)}) copy-start(f32[512,128]{1,0:T(8,128)} %get-tuple-element.5) | copy-start | bytes 786436

commit v4 on v3

--- a/solution.py
+++ b/solution.py
@@ -33,7 +33,13 @@
     return lax.dot_general(left, right, NT, preferred_element_type=F32)
 
 
-def communicate(u_in, l_in, buf, ush, loc, sems):
+def prepare(ref, turned, left):
+    value = ref[...].T
+    turned[...] = value
+    left[...] = left_form(value)
+
+
+def communicate(u_in, l_in, buf, ush, loc, low_t, low_l, up_t, up_l, sems):
     blk = lax.axis_index("blk")
     y = lax.axis_index("col")
     z, x, c = blk // 8, (blk // 2) % 4, blk % 2
@@ -263,18 +269,20 @@
     def _():
         ush[...] = jnp.zeros_like(ush)
 
+    local_l.wait()
+    prepare(loc, low_t, low_l)
     for d in (3, 1, 2):
         took_a(d)
+
+    @pl.when(blk > 0)
+    def _():
+        arrived(ush, sems["sh_r"])
+
+    prepare(ush, up_t, up_l)
     for j in (0, 3, 1, 2):
         took_b(j, 1, "fp_r")
         took_b(j, 3, "fm_r")
         took_b(j, 2, "hp_r")
-
-    local_l.wait()
-
-    @pl.when(blk > 0)
-    def _():
-        arrived(ush, sems["sh_r"])
 
     e = 1 - c
     pa, pb = x + e * (y - x), y + e * (x - y)
@@ -339,7 +347,7 @@
     finish()
 
 
-def compute(buf, ush, loc, u_out, l_out, n_l, n_r, g_l, h_f, h_l, m_r, k_l, k_n, k_t, d_r):
+def compute(buf, low_t, low_l, up_t, up_l, u_out, l_out, n_l, n_r, g_l, h_f, h_l, m_r, k_l, k_n, k_t, d_r):
     rows = lax.broadcasted_iota(jnp.int32, (B, W), 0)
     cols = lax.broadcasted_iota(jnp.int32, (B, W), 1)
     total = jnp.zeros((1, 1), F32)
@@ -366,7 +374,7 @@
         hi, lo = split(buf[1, y])
         put_left(g_l, whole, hi, lo, at)
 
-    step = 256
+    step = 512
 
     def first(i, carry):
         at = pl.multiple_of(i * step, step)
@@ -408,10 +416,8 @@
 
     lax.fori_loop(0, B // step, third, 0)
 
-    low = loc[...].T
-    up = ush[...].T
-    mixed = up - dot_nn(left_form(low), k_n[...])
-    rest = low - dot_nt(left_form(up), k_t[...])
+    mixed = up_t[...] - dot_nn(low_l[...], k_n[...])
+    rest = low_t[...] - dot_nt(up_l[...], k_t[...])
     pulled = dot_nt(left_form(mixed), k_t[...])
     both = jnp.concatenate([rest, pulled], axis=0)
     part = 0.3125 * both + 0.0625 * dot_nn(left_form(both), d_r[...])
@@ -433,9 +439,9 @@
 
 
 def kernel(u_in, l_in, u_out, l_out, buf, ush, loc, *rest):
-    mats, sems = rest[:10], dict(zip(SEMS, rest[10:]))
-    communicate(u_in, l_in, buf, ush, loc, sems)
-    compute(buf, ush, loc, u_out, l_out, *mats)
+    own, mats, sems = rest[:4], rest[4:14], dict(zip(SEMS, rest[14:]))
+    communicate(u_in, l_in, buf, ush, loc, *own, sems)
+    compute(buf, *own, u_out, l_out, *mats)
 
 
 def shards(upper_row, lower_row):
@@ -450,6 +456,7 @@
         out_specs=[pl.BlockSpec(memory_space=pltpu.VMEM)] * 2,
         scratch_shapes=[
             pltpu.VMEM((2, 4, B, W), F32), pltpu.VMEM((B, W), F32), pltpu.VMEM((B, W), F32),
+            *[pltpu.VMEM((W, B), F32), pltpu.VMEM((W, 3 * B), BF16)] * 2,
             cat_l, cat_r, cat_l, pltpu.VMEM((B, B), F32), cat_l, cat_r, cat_l, cat_r, cat_l, cat_r,
             *sems,
         ],

time: 47.2 us -> 45.3 us (0.960)
  Pallas kernels: 44 us -> 42.1 us
    pallas_call x1, Pallas kernels: 44 us -> 42.1 us  [shards(): pl.pallas_call(kernel, out_shape=(shape, shape), in_specs=[pl.BlockSpec(m...]
where the time goes in v4:
time: 45.3 us; the launch traced here: 45.2 us
  Pallas kernels  42.1 us (93%)
  local copies, waits for them, and re-layouts  2.42 us (5%)
  between operations  0.65 us (1%)
    pallas_call x1, Pallas kernels, shards(): pl.pallas_call(kernel, out_shape=(shape, shape), in_specs=[pl.BlockSpec(m...  42.1 us
    unnamed x4, local copies, waits for them, and re-layouts  2.42 us

profile of v4, /device:TPU:225, one launch (start us, length us, event | category | flops | bytes accessed | tf_op | source)
XLA Modules:
  0.0 45.2 jit_solution(15341262777190310797)
XLA Ops:
  0.6 42.1 %schur.1 = (f32[512,128]{1,0:T(8,128)}, f32[512,128]{1,0:T(8,128)}) custom-call(f32[512,128]{1,0:T(8,128)} %bitcast.8, f32[512,128]{1,0:T(8,128)} %bitcast.9), custom_call_target="tpu_custom_call" | custom-call | tf_op jit(solution)/shard_map/schur/pallas_call | solution.py:452
  42.7 0.0 copy-start
  42.8 1.7 %copy.8 = f32[512,1,128]{2,1,0:T(1,128)} copy(f32[512,1,128]{2,1,0:T(1,128)} %bitcast.11) | data formatting | bytes 524288
  44.5 0.0 copy-done
  44.5 0.7 %copy.9 = f32[512,1,128]{2,1,0:T(1,128)} copy(f32[512,1,128]{2,1,0:T(1,128)S(1)} %bitcast.10) | data formatting | bytes 524288
Async XLA Ops:
  42.7 1.7 %copy-start = (f32[512,128]{1,0:T(8,128)S(1)}, f32[512,128]{1,0:T(8,128)}, u32[]{:S(2)}) copy-start(f32[512,128]{1,0:T(8,128)} %get-tuple-element.5) | copy-start | bytes 786436

commit v5 on v4

--- a/solution.py
+++ b/solution.py
@@ -444,14 +444,17 @@
     compute(buf, *own, u_out, l_out, *mats)
 
 
+def hold(value):
+    return pltpu.with_memory_space_constraint(value.reshape(B, W), pltpu.HBM)
+
+
 def shards(upper_row, lower_row):
-    shape = jax.ShapeDtypeStruct((B, W), F32)
     cat_l, cat_r = pltpu.VMEM((B, 3 * B), BF16), pltpu.VMEM((3 * B, B), BF16)
     kinds = {REG: pltpu.SemaphoreType.REGULAR, REG16: pltpu.SemaphoreType.REGULAR((16,))}
     sems = [kinds[s] if s in kinds else pltpu.SemaphoreType.DMA(s) for s in SEMS.values()]
     new_upper, new_lower = pl.pallas_call(
         kernel,
-        out_shape=(shape, shape),
+        out_shape=(pltpu.VMEM((B, W), F32), pltpu.VMEM((B, W), F32)),
         in_specs=[pl.BlockSpec(memory_space=pl.ANY)] * 2,
         out_specs=[pl.BlockSpec(memory_space=pltpu.VMEM)] * 2,
         scratch_shapes=[
@@ -464,7 +467,7 @@
             collective_id=0, has_side_effects=True, vmem_limit_bytes=56 * 1024 * 1024
         ),
         name="schur",
-    )(upper_row.reshape(B, W), lower_row.reshape(B, W))
+    )(hold(upper_row), hold(lower_row))
     return new_upper.reshape(B, 1, W), new_lower.reshape(B, 1, W)
 
 

time: 45.3 us -> 43.6 us (0.962)
  local copies, waits for them, and re-layouts: 2.42 us -> 1.41 us
  Pallas kernels: 42.1 us -> 41.4 us
    unnamed x4 -> x2, local copies, waits for them, and re-layouts: 2.42 us -> 1.41 us
    pallas_call x1, Pallas kernels: 42.1 us -> 41.4 us  [shards(): pl.pallas_call(kernel, out_shape=(pltpu.VMEM((B, W), F32), pltpu.VMEM((B,...]
where the time goes in v5:
time: 43.6 us; the launch traced here: 43.5 us
  Pallas kernels  41.4 us (95%)
  local copies, waits for them, and re-layouts  1.41 us (3%)
  between operations  0.64 us (1%)
    pallas_call x1, Pallas kernels, shards(): pl.pallas_call(kernel, out_shape=(pltpu.VMEM((B, W), F32), pltpu.VMEM((B,...  41.4 us
    unnamed x2, local copies, waits for them, and re-layouts  1.41 us

profile of v5, /device:TPU:225, one launch (start us, length us, event | category | flops | bytes accessed | tf_op | source)
XLA Modules:
  0.0 43.5 jit_solution(14092026868356414902)
XLA Ops:
  0.6 41.4 %schur.1 = (f32[512,128]{1,0:T(8,128)S(1)}, f32[512,128]{1,0:T(8,128)S(1)}) custom-call(f32[512,128]{1,0:T(8,128)} %bitcast.10, f32[512,128]{1,0:T(8,128)} %bitcast.11), custom_call_target="tpu_custom_call" | custom-call | tf_op jit(solution)/shard_map/schur/pallas_call | solution.py:455
  42.1 0.7 %copy.8 = f32[512,1,128]{2,1,0:T(1,128)} copy(f32[512,1,128]{2,1,0:T(1,128)S(1)} %bitcast.9) | data formatting | bytes 524288
  42.8 0.7 %copy.9 = f32[512,1,128]{2,1,0:T(1,128)} copy(f32[512,1,128]{2,1,0:T(1,128)S(1)} %bitcast.8) | data formatting | bytes 524288

commit v6 on v5

--- a/solution.py
+++ b/solution.py
@@ -417,8 +417,8 @@
     lax.fori_loop(0, B // step, third, 0)
 
     mixed = up_t[...] - dot_nn(low_l[...], k_n[...])
-    rest = low_t[...] - dot_nt(up_l[...], k_t[...])
-    pulled = dot_nt(left_form(mixed), k_t[...])
+    pair = dot_nt(jnp.concatenate([up_l[...], left_form(mixed)], axis=0), k_t[...])
+    rest, pulled = low_t[...] - pair[:W], pair[W:]
     both = jnp.concatenate([rest, pulled], axis=0)
     part = 0.3125 * both + 0.0625 * dot_nn(left_form(both), d_r[...])
     part = 0.375 * both + dot_nn(left_form(part), d_r[...])

time: 43.6 us -> 43.1 us (0.989)
  Pallas kernels: 41.4 us -> 40.9 us
    pallas_call x1, Pallas kernels: 41.4 us -> 40.9 us  [shards(): pl.pallas_call(kernel, out_shape=(pltpu.VMEM((B, W), F32), pltpu.VMEM((B,...]
where the time goes in v6:
time: 43.1 us; the launch traced here: 42.9 us
  Pallas kernels  40.9 us (95%)
  local copies, waits for them, and re-layouts  1.41 us (3%)
  between operations  0.64 us (1%)
    pallas_call x1, Pallas kernels, shards(): pl.pallas_call(kernel, out_shape=(pltpu.VMEM((B, W), F32), pltpu.VMEM((B,...  40.9 us
    unnamed x2, local copies, waits for them, and re-layouts  1.41 us

profile of v6, /device:TPU:225, one launch (start us, length us, event | category | flops | bytes accessed | tf_op | source)
XLA Modules:
  0.0 42.9 jit_solution(7353399484554192603)
XLA Ops:
  0.6 40.9 %schur.1 = (f32[512,128]{1,0:T(8,128)S(1)}, f32[512,128]{1,0:T(8,128)S(1)}) custom-call(f32[512,128]{1,0:T(8,128)} %bitcast.10, f32[512,128]{1,0:T(8,128)} %bitcast.11), custom_call_target="tpu_custom_call" | custom-call | tf_op jit(solution)/shard_map/schur/pallas_call | solution.py:455
  41.5 0.7 %copy.8 = f32[512,1,128]{2,1,0:T(1,128)} copy(f32[512,1,128]{2,1,0:T(1,128)S(1)} %bitcast.9) | data formatting | bytes 524288
  42.2 0.7 %copy.9 = f32[512,1,128]{2,1,0:T(1,128)} copy(f32[512,1,128]{2,1,0:T(1,128)S(1)} %bitcast.8) | data formatting | bytes 524288

commit v7 on v6

--- a/solution.py
+++ b/solution.py
@@ -380,10 +380,11 @@
         at = pl.multiple_of(i * step, step)
         span = pl.ds(at, step)
         g = jnp.concatenate([buf[1, y, span, :] for y in range(4)], axis=1)
-        h = g + dot_nn(g_l[span, :], n_r[...])
+        pair = dot_nn(jnp.concatenate([g_l[span, :], n_l[span, :]], axis=0), n_r[...])
+        h = g + pair[:step]
         h_f[span, :] = h
         h_l[span, :] = left_form(h)
-        hi, lo = split(dot_nn(n_l[span, :], n_r[...]))
+        hi, lo = split(pair[step:])
         m_r[span, :] = hi
         m_r[pl.ds(B + at, step), :] = hi
         m_r[pl.ds(2 * B + at, step), :] = lo

time: 43.1 us -> 43 us (level)
  no operation moved by 1% of the time
where the time goes in v7:
time: 43 us; the launch traced here: 42.9 us
  Pallas kernels  40.8 us (95%)
  local copies, waits for them, and re-layouts  1.41 us (3%)
  between operations  0.64 us (1%)
    pallas_call x1, Pallas kernels, shards(): pl.pallas_call(kernel, out_shape=(pltpu.VMEM((B, W), F32), pltpu.VMEM((B,...  40.8 us
    unnamed x2, local copies, waits for them, and re-layouts  1.41 us

profile of v7, /device:TPU:225, one launch (start us, length us, event | category | flops | bytes accessed | tf_op | source)
XLA Modules:
  0.0 42.9 jit_solution(14067972195362709285)
XLA Ops:
  0.6 40.8 %schur.1 = (f32[512,128]{1,0:T(8,128)S(1)}, f32[512,128]{1,0:T(8,128)S(1)}) custom-call(f32[512,128]{1,0:T(8,128)} %bitcast.10, f32[512,128]{1,0:T(8,128)} %bitcast.11), custom_call_target="tpu_custom_call" | custom-call | tf_op jit(solution)/shard_map/schur/pallas_call | solution.py:456
  41.5 0.7 %copy.8 = f32[512,1,128]{2,1,0:T(1,128)} copy(f32[512,1,128]{2,1,0:T(1,128)S(1)} %bitcast.9) | data formatting | bytes 524288
  42.2 0.7 %copy.9 = f32[512,1,128]{2,1,0:T(1,128)} copy(f32[512,1,128]{2,1,0:T(1,128)S(1)} %bitcast.8) | data formatting | bytes 524288
